TPU v7x, 32 devices: a whole 2x2x4 slice. The times are simulated.
32 devices in a mesh: server: 16 (over z, x, core), helper: 2 (over y).
Axes of the slice: x: 2, y: 2, z: 4, core: 2. Of those that a mesh axis runs over, the one named last changes fastest.
Arguments:
- hidden_in: bfloat16 [512, 4, 4096], P('server', None, 'helper'), may hold values from -6 to 6
- base_out: bfloat16 [512, 4, 4096], P('server', None, 'helper'), may hold values from -6 to 6
- adapter_ids: int32 [512], P('server'), may hold values from 0 to 383, as said below
- left_blocks: bfloat16 [384, 64, 4096], P('server', 'helper'), may hold values from -0.75 to 0.75
- right_blocks: bfloat16 [384, 64, 4096], P('server', 'helper'), may hold values from -0.75 to 0.75
- down_rank: bfloat16 [384, 4096, 16], P('server', 'helper'), may hold values from -0.09375 to 0.09375
- up_rank: bfloat16 [384, 16, 4096], P('server', None, 'helper'), may hold values from -1.5 to 1.5
Outputs:
- adapted: bfloat16 [512, 4, 4096], P('server', None, 'helper')
Inputs may be any that keep to these rules, and one draw needn't show every extreme that they name: `adapter_ids`: of the requests of one server group (aligned blocks of 32), at most 2 name adapters of one owner, the owner of adapter a being a // 24; in every draw some owner gets exactly 2 from every group.
All inputs are finite; a program needn't handle non-finite values.
Results may differ from a plain program's by a relative error of at most 0.0059.
Values may be sent and summed in bfloat16 or wider, within the bound.
A program may use at most 64 MiB of HBM per device.

v0:
```python
import jax
import jax.numpy as jnp
from jax import lax
from jax.sharding import PartitionSpec as P

BLOCK = 64
CAP = 2


def local(hidden_in, base_out, adapter_ids, left_blocks, right_blocks, down_rank, up_rank):
    servers = lax.axis_size("server")
    requests, positions, width_here = hidden_in.shape
    adapters_here = left_blocks.shape[0]
    blocks_here = left_blocks.shape[1]
    block_size = BLOCK
    rank_width = down_rank.shape[2]
    slot_total = servers * CAP
    owners = adapter_ids // adapters_here
    local_id = adapter_ids % adapters_here
    owner_hits = (owners[:, None] == jnp.arange(servers)[None, :]).astype(jnp.int32)
    earlier = jnp.cumsum(owner_hits, axis=0) - owner_hits
    target = owners * CAP + jnp.sum(earlier * owner_hits, axis=1)
    placing = (jnp.arange(slot_total)[:, None] == target[None, :]).astype(jnp.bfloat16)
    packed = jnp.dot(
        placing,
        hidden_in.reshape(requests, positions * width_here),
        preferred_element_type=jnp.float32,
    ).astype(jnp.bfloat16)
    labels = jnp.dot(
        placing, (local_id + 1).astype(jnp.bfloat16), preferred_element_type=jnp.float32
    ).astype(jnp.bfloat16)
    arrived, arrived_labels = (
        lax.all_to_all(
            packed.reshape(servers, CAP, positions, width_here),
            "server",
            split_axis=0,
            concat_axis=0,
            tiled=True,
        ),
        lax.all_to_all(
            labels.reshape(servers, CAP), "server", split_axis=0, concat_axis=0, tiled=True
        ),
    )
    row_count = slot_total * positions
    flat_rows = arrived.reshape(row_count, width_here)
    block_rows = arrived.reshape(row_count, blocks_here, block_size)
    slot_labels = arrived_labels.reshape(slot_total, 1).astype(jnp.int32)
    row_labels = jnp.broadcast_to(slot_labels, (slot_total, positions)).reshape(row_count)
    numbers = jnp.arange(adapters_here, dtype=jnp.int32)

    def first_factor(carry, inputs):
        mixed_acc, rank_acc = carry
        left_flat, down_tile, number = inputs
        left_tile = left_flat.reshape(blocks_here, block_size, block_size)
        selected = row_labels == number + 1
        mixed = jnp.einsum(
            "rij,ikj->rik", block_rows, left_tile, preferred_element_type=jnp.float32
        ).astype(jnp.bfloat16)
        mixed_acc = jnp.where(selected[:, None, None], mixed, mixed_acc)
        partial_rank = jnp.dot(flat_rows, down_tile, preferred_element_type=jnp.float32)
        rank_acc = jnp.where(selected[:, None], partial_rank, rank_acc)
        return ((mixed_acc, rank_acc), None)

    start_mixed = jnp.zeros((row_count, blocks_here, block_size), jnp.bfloat16)
    start_rank = jnp.zeros((row_count, rank_width), jnp.float32)
    (mixed_rows, rank_partial), ignored = lax.scan(
        first_factor, (start_mixed, start_rank), (left_blocks, down_rank, numbers)
    )
    turned = lax.all_to_all(mixed_rows, "helper", split_axis=2, concat_axis=1, tiled=True)
    rank_sum = lax.psum(rank_partial, "helper")
    rank_proj = rank_sum.astype(jnp.bfloat16)
    columns_here = turned.shape[2]

    def second_factor(carry, inputs):
        right_acc, low_acc = carry
        right_flat, up_tile, number = inputs
        right_tile = right_flat.reshape(right_flat.shape[0], block_size, block_size)
        selected = row_labels == number + 1
        right_out = jnp.einsum(
            "rik,kmi->rmk", turned, right_tile, preferred_element_type=jnp.float32
        ).astype(jnp.bfloat16)
        right_acc = jnp.where(selected[:, None, None], right_out, right_acc)
        low_out = jnp.dot(rank_proj, up_tile, preferred_element_type=jnp.float32).astype(
            jnp.bfloat16
        )
        low_acc = jnp.where(selected[:, None], low_out, low_acc)
        return ((right_acc, low_acc), None)

    start_right = jnp.zeros((row_count, block_size, columns_here), jnp.bfloat16)
    start_low = jnp.zeros((row_count, width_here), jnp.bfloat16)
    (right_rows, rank_rows), ignored = lax.scan(
        second_factor, (start_right, start_low), (right_blocks, up_rank, numbers)
    )
    monarch_rows = lax.all_to_all(
        right_rows, "helper", split_axis=1, concat_axis=2, tiled=True
    ).reshape(row_count, width_here)
    summed_rows = (monarch_rows.astype(jnp.float32) + rank_rows.astype(jnp.float32)).astype(
        jnp.bfloat16
    )
    back_delta = lax.all_to_all(
        summed_rows.reshape(servers, CAP, positions, width_here),
        "server",
        split_axis=0,
        concat_axis=0,
        tiled=True,
    )
    flat_buffer = back_delta.reshape(slot_total, -1)
    delta = (
        jnp.einsum("sr,sc->rc", placing, flat_buffer, preferred_element_type=jnp.float32)
        .astype(jnp.bfloat16)
        .reshape(requests, positions, width_here)
    )
    total = base_out.astype(jnp.float32) + delta.astype(jnp.float32)
    return total.astype(jnp.bfloat16)


def solution(mesh):
    in_specs = (
        P("server", None, "helper"),
        P("server", None, "helper"),
        P("server"),
        P("server", "helper", None),
        P("server", "helper", None),
        P("server", "helper", None),
        P("server", None, "helper"),
    )
    out_specs = P("server", None, "helper")
    return jax.shard_map(local, mesh=mesh, in_specs=in_specs, out_specs=out_specs, check_vma=False)
```

profile of v0, /device:TPU:0, one launch (start us, length us, event | category | flops | bytes accessed | tf_op | source)
XLA Modules:
  0.0 309.8 jit_solution(3103036120894097334)
XLA Ops:
  3.1 7.4 %all-to-all-start = ((bf16[16,1,2]{2,1,0:T(2,128)(2,1)}), bf16[16,1,2]{2,1,0:T(2,128)(2,1)S(1)}, u32[]{:S(2)}, u32[]{:S(2)}) async-start(bf16[16,1,2]{2,1,0:T(2,128)(2,1)} %all_to_all.41), calls=%async_computation | async-start | bytes 16384 | tf_op jit(solution)/shard_map/all_to_all | solution.py:40
  10.5 1.3 copy.22
  12.2 1.2 reshape.73
  13.3 3.6 %all-to-all-done = bf16[16,1,2]{2,1,0:T(2,128)(2,1)S(1)} async-done(((bf16[16,1,2]{2,1,0:T(2,128)(2,1)}), bf16[16,1,2]{2,1,0:T(2,128)(2,1)S(1)}, u32[]{:S(2)}, u32[]{:S(2)}) %all-to-all-start) | async-done | bytes 96 | tf_op jit(solution)/shard_map/all_to_all | solution.py:40
  17.0 3.6 %all-to-all-start.1 = ((bf16[16,2,4,2048]{3,2,1,0:T(4,128)(2,1)}), bf16[16,2,4,2048]{3,2,1,0:T(4,128)(2,1)S(1)}, u32[]{:S(2)}, u32[]{:S(2)}) async-start(bf16[16,2,4,2048]{3,2,1,0:T(4,128)(2,1)} %reshape.73), calls=%async_computation.1 | async-start | bytes 1048576 | tf_op jit(solution)/shard_map/all_to_all | solution.py:33
  20.7 14.1 %all-to-all-done.1 = bf16[16,2,4,2048]{3,2,1,0:T(4,128)(2,1)S(1)} async-done(((bf16[16,2,4,2048]{3,2,1,0:T(4,128)(2,1)}), bf16[16,2,4,2048]{3,2,1,0:T(4,128)(2,1)S(1)}, u32[]{:S(2)}, u32[]{:S(2)}) %all-to-all-start.1) | async-done | bytes 524320 | tf_op jit(solution)/shard_map/all_to_all | solution.py:33
  35.6 1.1 copy.16
  36.8 109.6 %while.26 = (s32[]{:T(128)}, bf16[128,32,64]{0,2,1:T(8,128)(2,1)S(1)}, f32[128,16]{0,1:T(8,128)S(1)}, s32[24]{0:T(128)S(1)}, bf16[24,32,4096]{2,1,0:T(8,128)(2,1...) while((s32[]{:T(128)}, ...), condition=%wide.region_3.4_spmd.clone, body=%wide.region_2.3_spmd.clone.sunk | while | flops 42733700 | bytes 3493024 | solution.py:66
  40.3 1.1 fusion.60
  42.9 1.0 constant_dynamic-slice_fusion.4
  44.9 1.1 fusion.60
  49.4 1.1 fusion.60
  54.0 1.1 fusion.60
  58.6 1.1 fusion.60
  63.2 1.1 fusion.60
  67.7 1.1 fusion.60
  72.3 1.1 fusion.60
  76.9 1.1 fusion.60
  81.4 1.1 fusion.60
  86.0 1.1 fusion.60
  90.6 1.1 fusion.60
  95.1 1.1 fusion.60
  99.7 1.1 fusion.60
  104.3 1.1 fusion.60
  108.8 1.1 fusion.60
  113.4 1.1 fusion.60
  118.0 1.1 fusion.60
  122.5 1.1 fusion.60
  127.1 1.1 fusion.60
  131.7 1.1 fusion.60
  136.2 1.1 fusion.60
  140.8 1.1 fusion.60
  145.4 1.1 fusion.60
  146.5 1.2 copy.17
  147.6 3.5 %all-to-all-start.2 = ((bf16[128,32,64]{0,1,2:T(8,128)(2,1)}), bf16[128,32,64]{0,1,2:T(8,128)(2,1)S(1)}, u32[]{:S(2)}, u32[]{:S(2)}) async-start(bf16[128,32,64]{0,1,2:T(8,128)(2,1)} %copy.17), calls=%async_computation.2 | async-start | bytes 1048576 | tf_op jit(solution)/shard_map/all_to_all | solution.py:69
  151.1 8.7 %psum.7 = bf16[128,16]{0,1:T(8,128)(2,1)S(1)} all-reduce(f32[128,16]{0,1:T(8,128)S(1)} %get-tuple-element.102), channel_id=1, replica_groups=mesh['server'=16,'helper'=2] {'helper'}, use_global_device_ids=true, to_apply=%region_4.5 | all-reduce | flops 2048 | bytes 12288 | tf_op jit(solution)/shard_map/psum | solution.py:70
  159.9 117.4 %while.27 = (s32[]{:T(128)}, bf16[128,64,32]{0,1,2:T(8,128)(2,1)S(1)}, bf16[128,2048]{0,1:T(8,128)(2,1)S(1)}, s32[24]{0:T(128)S(1)}, bf16[24,32,4096]{2,1,0:T(8,...) while((s32[]{:T(128)}, ...), condition=%wide.region_6.7_spmd.clone, body=%wide.region_5.6_spmd.clone.sunk | while | flops 43516036 | bytes 4005024 | solution.py:91
  163.4 1.4 fusion.66
  168.3 1.4 fusion.66
  173.2 1.4 fusion.66
  178.1 1.4 fusion.66
  183.0 1.4 fusion.66
  187.9 1.4 fusion.66
  192.8 1.4 fusion.66
  197.6 1.4 fusion.66
  202.5 1.4 fusion.66
  207.4 1.4 fusion.66
  212.3 1.4 fusion.66
  217.2 1.4 fusion.66
  222.1 1.4 fusion.66
  227.0 1.4 fusion.66
  231.9 1.4 fusion.66
  236.8 1.4 fusion.66
  241.7 1.4 fusion.66
  246.6 1.4 fusion.66
  251.5 1.4 fusion.66
  256.4 1.4 fusion.66
  261.3 1.4 fusion.66
  266.1 1.4 fusion.66
  271.0 1.4 fusion.66
  275.9 1.4 fusion.66
  277.7 10.1 %all_to_all.47 = bf16[128,64,32]{0,2,1:T(8,128)(2,1)S(1)} all-to-all(bf16[128,64,32]{0,2,1:T(8,128)(2,1)S(1)} %copy.19), channel_id=1, replica_groups=mesh['server'=16,'helper'=2] {'helper'}, dimensions={1} | all-to-all | bytes 1048576 | tf_op jit(solution)/shard_map/all_to_all | solution.py:94
  288.6 18.7 %all_to_all.48 = bf16[16,2,4,2048]{3,2,1,0:T(4,128)(2,1)S(1)} all-to-all(bf16[16,2,4,2048]{3,2,1,0:T(4,128)(2,1)S(1)} %reshape.76), channel_id=1, replica_groups=mesh['server'=16,'helper'=2] {'server'}, dimensions={0} | all-to-all | bytes 1048576 | tf_op jit(solution)/shard_map/all_to_all | solution.py:100
  308.7 1.1 add_convert_fusion
  (366 shorter events, 139.9 us)
Async XLA Ops:
  3.1 13.8 %all-to-all-start = ((bf16[16,1,2]{2,1,0:T(2,128)(2,1)}), bf16[16,1,2]{2,1,0:T(2,128)(2,1)S(1)}, u32[]{:S(2)}, u32[]{:S(2)}) async-start(bf16[16,1,2]{2,1,0:T(2,128)(2,1)} %all_to_all.41), calls=%async_computation | async-start | bytes 16384 | tf_op jit(solution)/shard_map/all_to_all | solution.py:40
  17.0 17.8 %all-to-all-start.1 = ((bf16[16,2,4,2048]{3,2,1,0:T(4,128)(2,1)}), bf16[16,2,4,2048]{3,2,1,0:T(4,128)(2,1)S(1)}, u32[]{:S(2)}, u32[]{:S(2)}) async-start(bf16[16,2,4,2048]{3,2,1,0:T(4,128)(2,1)} %reshape.73), calls=%async_computation.1 | async-start | bytes 1048576 | tf_op jit(solution)/shard_map/all_to_all | solution.py:33
  147.6 12.2 %all-to-all-start.2 = ((bf16[128,32,64]{0,1,2:T(8,128)(2,1)}), bf16[128,32,64]{0,1,2:T(8,128)(2,1)S(1)}, u32[]{:S(2)}, u32[]{:S(2)}) async-start(bf16[128,32,64]{0,1,2:T(8,128)(2,1)} %copy.17), calls=%async_computation.2 | async-start | bytes 1048576 | tf_op jit(solution)/shard_map/all_to_all | solution.py:69
  307.6 1.1 copy-start
where the time goes:
time: 314 us; the launch traced here: 310 us
  local copies, waits for them, and re-layouts  118 us (38%)
  matrix products  85.6 us (27%)
  blocking collectives  37.5 us (12%)
  loops' own time  33.1 us (11%)
  waiting for transfers between devices  17.7 us (6%)
  starting transfers between devices  14.4 us (5%)
  other arithmetic  3.48 us (1%)
    dynamic_slice x96, local copies, waits for them, and re-layouts, local(): lax.scan(first_factor, (start_mixed, start_rank), (left_blocks, down_rank...  75.2 us
    dot_general x24, matrix products, second_factor(): jnp.dot(rank_proj, up_tile, preferred_element_type=jnp.float32)  34 us
    dot_general x24, matrix products, first_factor(): jnp.dot(flat_rows, down_tile, preferred_element_type=jnp.float32)  26.1 us
    all_to_all x1, blocking collectives, local(): lax.all_to_all(summed_rows.reshape(servers, CAP, positions, width_here),...  18.7 us
    another operation x1, loops' own time, local(): lax.scan(second_factor, (start_right, start_low), (right_blocks, up_rank,...  16.7 us
    another operation x1, loops' own time, local(): lax.scan(first_factor, (start_mixed, start_rank), (left_blocks, down_rank...  16.4 us
    all_to_all x1, waiting for transfers between devices, local(): lax.all_to_all(packed.reshape(servers, CAP, positions, width_here), 'serv...  14.1 us
    reshape x24, local copies, waits for them, and re-layouts, first_factor(): left_tile = left_flat.reshape(blocks_here, block_size, block_size)  12.8 us
  transfers between devices with their start and end apart: 3, of which 2 were waited for; matrix products, arithmetic and copies ran while one was open for 1% of the time, Pallas kernels for 0%

commit v1 on v0

--- a/solution.py
+++ b/solution.py
@@ -1,13 +1,17 @@
+import functools
+
 import jax
 import jax.numpy as jnp
 from jax import lax
+from jax.experimental import pallas as pl
+from jax.experimental.pallas import tpu as pltpu
 from jax.sharding import PartitionSpec as P
 
 BLOCK = 64
 CAP = 2
 
 
-def local(hidden_in, base_out, adapter_ids, left_blocks, right_blocks, down_rank, up_rank):
+def plain(hidden_in, base_out, adapter_ids, left_blocks, right_blocks, down_rank, up_rank):
     servers = lax.axis_size("server")
     requests, positions, width_here = hidden_in.shape
     adapters_here = left_blocks.shape[0]
@@ -114,6 +118,403 @@
     return total.astype(jnp.bfloat16)
 
 
+LANES = 128
+GROUP = 4
+MESH = pl.DeviceIdType.MESH
+NT = (((1,), (1,)), ((), ()))
+
+
+def greet(axis, count):
+    me = lax.axis_index(axis)
+    barrier = pltpu.get_barrier_semaphore()
+    for step in range(1, count):
+        peer = lax.rem(me + step, count)
+        pl.semaphore_signal(barrier, inc=1, device_id={axis: peer}, device_id_type=MESH)
+    pl.semaphore_wait(barrier, count - 1)
+
+
+def lanes_of(shape, dim=1):
+    return lax.broadcasted_iota(jnp.int32, shape, dim)
+
+
+def scatter_kernel(count, inv, hid, lab, out, lab_out, packed, send, recv, lab_send, lab_recv):
+    me = lax.axis_index("server")
+    cap = packed.shape[1]
+    for dst in range(count):
+        for c in range(cap):
+            packed[dst, c] = hid[inv[dst * cap + c]]
+    greet("server", count)
+    copies = []
+    for step in range(1, count):
+        peer = lax.rem(me + step, count)
+        for src, dst, s, r in (
+            (lab, lab_out, lab_send, lab_recv),
+            (packed, out, send, recv),
+        ):
+            copy = pltpu.make_async_remote_copy(
+                src_ref=src.at[peer],
+                dst_ref=dst.at[me],
+                send_sem=s.at[step],
+                recv_sem=r.at[step],
+                device_id={"server": peer},
+                device_id_type=MESH,
+            )
+            copy.start()
+            copies.append(copy)
+    out[me] = packed[me]
+    lab_out[me] = lab[me]
+    for copy in copies:
+        copy.wait()
+
+
+def first_kernel(labels, hid, *refs):
+    lefts, downs, (mixed, rank) = refs[:GROUP], refs[GROUP : 2 * GROUP], refs[2 * GROUP :]
+    helpers, _, rows_out, wide = mixed.shape
+    blocks, flat = lefts[0].shape[1:]
+    rank_width = downs[0].shape[1]
+    rows = hid.shape[1]
+    positions = rank.shape[1]
+    tiles = rows // positions
+    low = lanes_of((rows, LANES)) < LANES // 2
+    lane = lanes_of((blocks, wide))
+    row = lanes_of((blocks, wide), 0)
+    keep = row == 2 * (lane % tiles) + (lane // rows) % 2
+    same = lanes_of((rows, wide), 0) % tiles == lanes_of((rows, wide)) // rank_width
+    fold = (
+        lanes_of((wide, LANES), 0) % rank_width == lanes_of((wide, LANES)) % rank_width
+    ).astype(jnp.bfloat16)
+    for g in range(GROUP):
+        x = hid[g]
+        xf = x.astype(jnp.float32)
+        turned = pltpu.roll(xf, LANES // 2, 1)
+        zero = jnp.zeros_like(xf)
+        stationary = jnp.concatenate(
+            [
+                jnp.where(low, xf, zero),
+                jnp.where(low, turned, zero),
+                jnp.where(low, zero, turned),
+                jnp.where(low, zero, xf),
+            ],
+            axis=0,
+        ).astype(jnp.bfloat16)
+        left = jnp.concatenate(
+            [lefts[g][0, :, k * LANES : (k + 1) * LANES] for k in range(flat // LANES)], axis=0
+        )
+        full = lax.dot_general(left, stationary, NT, preferred_element_type=jnp.float32)
+        full = full.reshape(flat // LANES, blocks, wide)
+        got = jnp.sum(jnp.where(keep[None], full, 0.0), axis=1).astype(jnp.bfloat16)
+        for h in range(helpers):
+            mixed[h, g] = got[h * rows_out : (h + 1) * rows_out]
+        down = jnp.concatenate(
+            [downs[g][0, :, t * LANES : (t + 1) * LANES] for t in range(tiles)], axis=0
+        )
+        part = lax.dot_general(x, down, NT, preferred_element_type=jnp.float32)
+        part = jnp.where(same, part, 0.0).reshape(positions, tiles, wide)
+        part = jnp.sum(part, axis=1)
+        high = part.astype(jnp.bfloat16)
+        rest = (part - high.astype(jnp.float32)).astype(jnp.bfloat16)
+        rank[g] = jnp.dot(high, fold, preferred_element_type=jnp.float32) + jnp.dot(
+            rest, fold, preferred_element_type=jnp.float32
+        )
+
+
+def swap_kernel(count, mixed, rank, weights, proj, got, got_rank, send, recv, rsend, rrecv):
+    me = lax.axis_index("helper")
+    slots, rows_out, wide = mixed.shape[1:]
+    greet("helper", count)
+    copies = []
+    for step in range(1, count):
+        peer = lax.rem(me + step, count)
+        for src, dst, s, r in ((rank, got_rank.at[me], rsend, rrecv), (mixed.at[peer], got.at[me], send, recv)):
+            copy = pltpu.make_async_remote_copy(
+                src_ref=src,
+                dst_ref=dst,
+                send_sem=s.at[step],
+                recv_sem=r.at[step],
+                device_id={"helper": peer},
+                device_id_type=MESH,
+            )
+            copy.start()
+            copies.append(copy)
+    got[me] = mixed[me]
+    got_rank[me] = rank[...]
+    for copy in copies:
+        copy.wait()
+    total = got_rank[0]
+    for h in range(1, count):
+        total = total + got_rank[h]
+    proj[...] = total.astype(jnp.bfloat16).astype(jnp.float32)
+    positions = rank.shape[1]
+    half = wide // 2
+    tiles = half // 2 // positions
+    src = lanes_of((wide, wide), 0)
+    dst = lanes_of((wide, wide))
+    block = 2 * (src % tiles) + (src // (half // 2)) % 2
+    picks = [
+        (
+            (dst // LANES == (dst // (LANES // 2)) % 2)
+            & (dst % (LANES // 2) == 2 * tiles * h + block)
+        ).astype(jnp.bfloat16)
+        for h in range(count)
+    ]
+    lane = lanes_of((slots * rows_out, wide))
+    code = (lane // half) * positions + (lane // tiles) % positions
+    rows = [got[h].reshape(slots * rows_out, wide).astype(jnp.float32) for h in range(count)]
+    for q in range(2 * positions):
+        acc = None
+        for h in range(count):
+            part = jnp.where(code == q, rows[h], 0.0).astype(jnp.bfloat16)
+            term = jnp.dot(part, picks[h], preferred_element_type=jnp.float32)
+            acc = term if acc is None else acc + term
+        acc = acc.astype(jnp.bfloat16)
+        for c in range(2):
+            at = (c * 2 * positions + q) * rows_out
+            weights[:, at : at + rows_out, :] = acc[:, c * LANES : (c + 1) * LANES].reshape(
+                slots, rows_out, LANES
+            )
+
+
+def second_kernel(labels, weights, proj, *refs):
+    rights, ups, (right_out, rank_out) = refs[:GROUP], refs[GROUP : 2 * GROUP], refs[2 * GROUP :]
+    helpers, _, rows_out, wide = right_out.shape
+    blocks, flat = rights[0].shape[1:]
+    rank_width = ups[0].shape[1]
+    positions = proj.shape[1]
+    rows = rank_out.shape[1]
+    tiles = rows // positions
+    lane = lanes_of((blocks, wide))
+    keep = lanes_of((blocks, wide), 0) == 2 * (lane % rows_out) + (lane // (rows_out * positions)) % 2
+    same = lanes_of((rows, wide), 0) % tiles == lanes_of((rows, wide)) // rank_width
+    for g in range(GROUP):
+        right = jnp.concatenate(
+            [rights[g][0, :, k * LANES : (k + 1) * LANES] for k in range(flat // LANES)], axis=0
+        )
+        full = lax.dot_general(right, weights[g], NT, preferred_element_type=jnp.float32)
+        full = full.reshape(flat // LANES, blocks, wide)
+        got = jnp.sum(jnp.where(keep[None], full, 0.0), axis=1).astype(jnp.bfloat16)
+        for h in range(helpers):
+            right_out[h, g] = got[h * rows_out : (h + 1) * rows_out]
+        p = proj[g]
+        tall = jnp.concatenate(
+            [jnp.broadcast_to(p[i : i + 1], (tiles, LANES)) for i in range(positions)], axis=0
+        )
+        tall = jnp.concatenate([tall] * (wide // LANES), axis=1)
+        tall = jnp.where(same, tall, 0.0).astype(jnp.bfloat16)
+        up = jnp.concatenate(
+            [ups[g][0, :, t * LANES : (t + 1) * LANES] for t in range(tiles)], axis=0
+        )
+        rank_out[g] = jnp.dot(tall, up, preferred_element_type=jnp.float32).astype(jnp.bfloat16)
+
+
+def gather_kernel(
+    helpers, count, tgt, right_out, rank_out, base, out, got, delta, back, hsend, hrecv, send, recv
+):
+    me = lax.axis_index("helper")
+    here = lax.axis_index("server")
+    slots, rows_out, wide = right_out.shape[1:]
+    cap = slots // count
+    positions = rank_out.shape[1] // rows_out
+    barrier = pltpu.get_barrier_semaphore()
+    for step in range(1, helpers):
+        peer = lax.rem(me + step, helpers)
+        pl.semaphore_signal(barrier, inc=1, device_id={"helper": peer}, device_id_type=MESH)
+    for step in range(1, count):
+        peer = lax.rem(here + step, count)
+        pl.semaphore_signal(barrier, inc=1, device_id={"server": peer}, device_id_type=MESH)
+    pl.semaphore_wait(barrier, helpers + count - 2)
+    copies = []
+    for step in range(1, helpers):
+        peer = lax.rem(me + step, helpers)
+        copy = pltpu.make_async_remote_copy(
+            src_ref=right_out.at[peer],
+            dst_ref=got.at[me],
+            send_sem=hsend.at[step],
+            recv_sem=hrecv.at[step],
+            device_id={"helper": peer},
+            device_id_type=MESH,
+        )
+        copy.start()
+        copies.append(copy)
+    got[me] = right_out[me]
+    for copy in copies:
+        copy.wait()
+    src = lanes_of((wide, LANES), 0)
+    dst = lanes_of((wide, LANES))
+    span = 2 * rows_out
+    number = 2 * (src % rows_out) + (src // (rows_out * positions)) % 2
+    picks = [
+        (
+            (src // (2 * rows_out * positions) == dst // (LANES // 2))
+            & (dst % (LANES // 2) == span * h + number)
+        ).astype(jnp.bfloat16)
+        for h in range(helpers)
+    ]
+    lane = lanes_of((slots * rows_out, wide))
+    code = (lane // rows_out) % positions
+    rows = [got[h].reshape(slots * rows_out, wide).astype(jnp.float32) for h in range(helpers)]
+    for p in range(positions):
+        acc = None
+        for h in range(helpers):
+            part = jnp.where(code == p, rows[h], 0.0).astype(jnp.bfloat16)
+            term = jnp.dot(part, picks[h], preferred_element_type=jnp.float32)
+            acc = term if acc is None else acc + term
+        low = rank_out[:, p * rows_out : (p + 1) * rows_out, :].reshape(slots * rows_out, LANES)
+        total = (acc + low.astype(jnp.float32)).astype(jnp.bfloat16)
+        delta[:, :, p * rows_out : (p + 1) * rows_out, :] = total.reshape(count, cap, rows_out, LANES)
+    copies = []
+    for step in range(1, count):
+        peer = lax.rem(here + step, count)
+        copy = pltpu.make_async_remote_copy(
+            src_ref=delta.at[peer],
+            dst_ref=back.at[here],
+            send_sem=send.at[step],
+            recv_sem=recv.at[step],
+            device_id={"server": peer},
+            device_id_type=MESH,
+        )
+        copy.start()
+        copies.append(copy)
+    back[here] = delta[here]
+    for copy in copies:
+        copy.wait()
+    for r in range(out.shape[0]):
+        t = tgt[r]
+        row = back[t // cap, t % cap]
+        out[r] = (base[r].astype(jnp.float32) + row.astype(jnp.float32)).astype(jnp.bfloat16)
+
+
+VM = pl.BlockSpec(memory_space=pltpu.VMEM)
+SM = pl.BlockSpec(memory_space=pltpu.SMEM)
+
+
+def local(hidden_in, base_out, adapter_ids, left_blocks, right_blocks, down_rank, up_rank):
+    servers = lax.axis_size("server")
+    helpers = lax.axis_size("helper")
+    requests, positions, width_here = hidden_in.shape
+    adapters_here, blocks_here, flat = left_blocks.shape
+    rank_width = down_rank.shape[2]
+    tiles = width_here // LANES
+    rows = positions * tiles
+    wide = 4 * rows
+    slots = servers * CAP
+    rows_out = flat // LANES // helpers
+    fits = (
+        2 * tiles == blocks_here
+        and rows_out == tiles
+        and wide == 2 * LANES
+        and tiles * rank_width == wide
+        and slots % GROUP == 0
+        and tiles % 16 == 0
+    )
+    if not fits:
+        return plain(
+            hidden_in, base_out, adapter_ids, left_blocks, right_blocks, down_rank, up_rank
+        )
+    bf16 = jnp.bfloat16
+    owners = adapter_ids // adapters_here
+    local_id = adapter_ids % adapters_here
+    number = jnp.arange(requests, dtype=jnp.int32)
+    earlier = (owners[:, None] == owners[None, :]) & (number[None, :] < number[:, None])
+    target = owners * CAP + jnp.sum(earlier.astype(jnp.int32), axis=1)
+    hit = jnp.arange(slots, dtype=jnp.int32)[:, None] == target[None, :]
+    inv = jnp.sum(jnp.where(hit, number[None, :], 0), axis=1)
+    labels = jnp.sum(jnp.where(hit, local_id[None, :], 0), axis=1)
+    lab = jnp.broadcast_to(
+        jnp.pad(labels.reshape(servers, CAP), ((0, 0), (0, LANES - CAP)))[:, None, :],
+        (servers, 8, LANES),
+    )
+    hid = hidden_in.reshape(requests, rows, LANES)
+    dma = pltpu.SemaphoreType.DMA
+    arrived, arrived_lab = pl.pallas_call(
+        functools.partial(scatter_kernel, servers),
+        out_shape=(
+            jax.ShapeDtypeStruct((servers, CAP, rows, LANES), bf16),
+            jax.ShapeDtypeStruct((servers, 8, LANES), jnp.int32),
+        ),
+        in_specs=[SM, VM, VM],
+        out_specs=(VM, VM),
+        scratch_shapes=[pltpu.VMEM((servers, CAP, rows, LANES), bf16)] + [dma((servers,))] * 4,
+        compiler_params=pltpu.CompilerParams(collective_id=0, has_side_effects=True),
+        name="scatter",
+    )(inv, hid, lab)
+    slot_labels = arrived_lab[:, 0, :CAP].reshape(slots)
+
+    def weight_specs(shape):
+        def spec(g):
+            return pl.BlockSpec((1,) + shape, lambda s, lab_ref: (lab_ref[s * GROUP + g], 0, 0))
+
+        return [spec(g) for g in range(GROUP)]
+
+    def group_spec(*shape):
+        return pl.BlockSpec((GROUP,) + shape, lambda s, lab_ref: (s, 0, 0))
+
+    def half_spec():
+        return pl.BlockSpec((helpers, GROUP, rows_out, wide), lambda s, lab_ref: (0, s, 0, 0))
+
+    half = jax.ShapeDtypeStruct((helpers, slots, rows_out, wide), bf16)
+    thin = jax.ShapeDtypeStruct((slots, positions, LANES), jnp.float32)
+    mixed, rank = pl.pallas_call(
+        first_kernel,
+        out_shape=(half, thin),
+        grid_spec=pltpu.PrefetchScalarGridSpec(
+            num_scalar_prefetch=1,
+            grid=(slots // GROUP,),
+            in_specs=[group_spec(rows, LANES)]
+            + weight_specs((blocks_here, flat))
+            + weight_specs((rank_width, width_here)),
+            out_specs=(half_spec(), group_spec(positions, LANES)),
+        ),
+        name="first",
+    )(
+        slot_labels,
+        arrived.reshape(slots, rows, LANES),
+        *([left_blocks] * GROUP),
+        *([jnp.swapaxes(down_rank, 1, 2)] * GROUP),
+    )
+    weights, proj = pl.pallas_call(
+        functools.partial(swap_kernel, helpers),
+        out_shape=(jax.ShapeDtypeStruct((slots, wide, LANES), bf16), thin),
+        in_specs=[VM, VM],
+        out_specs=(VM, VM),
+        scratch_shapes=[
+            pltpu.VMEM((helpers, slots, rows_out, wide), bf16),
+            pltpu.VMEM((helpers, slots, positions, LANES), jnp.float32),
+        ]
+        + [dma((helpers,))] * 4,
+        compiler_params=pltpu.CompilerParams(collective_id=1, has_side_effects=True),
+        name="swap",
+    )(mixed, rank)
+    right_out, rank_out = pl.pallas_call(
+        second_kernel,
+        out_shape=(half, jax.ShapeDtypeStruct((slots, rows, LANES), bf16)),
+        grid_spec=pltpu.PrefetchScalarGridSpec(
+            num_scalar_prefetch=1,
+            grid=(slots // GROUP,),
+            in_specs=[group_spec(wide, LANES), group_spec(positions, LANES)]
+            + weight_specs((blocks_here, flat))
+            + weight_specs((rank_width, width_here)),
+            out_specs=(half_spec(), group_spec(rows, LANES)),
+        ),
+        name="second",
+    )(slot_labels, weights, proj, *([right_blocks] * GROUP), *([up_rank] * GROUP))
+    out = pl.pallas_call(
+        functools.partial(gather_kernel, helpers, servers),
+        out_shape=jax.ShapeDtypeStruct((requests, rows, LANES), bf16),
+        in_specs=[SM, VM, VM, VM],
+        out_specs=VM,
+        scratch_shapes=[
+            pltpu.VMEM((helpers, slots, rows_out, wide), bf16),
+            pltpu.VMEM((servers, CAP, rows, LANES), bf16),
+            pltpu.VMEM((servers, CAP, rows, LANES), bf16),
+        ]
+        + [dma((helpers,))] * 2
+        + [dma((servers,))] * 2,
+        compiler_params=pltpu.CompilerParams(collective_id=2, has_side_effects=True),
+        name="gather",
+    )(target, right_out, rank_out, base_out.reshape(requests, rows, LANES))
+    return out.reshape(requests, positions, width_here)
+
+
 def solution(mesh):
     in_specs = (
         P("server", None, "helper"),

time: 314 us -> 94.8 us (0.30)
  local copies, waits for them, and re-layouts: 118 us -> 7.52 us
  matrix products: 85.6 us -> 0 us
  Pallas kernels: 0 us -> 84 us
  blocking collectives: 37.5 us -> 0 us
  loops' own time: 33.1 us -> 0 us
  waiting for transfers between devices: 17.7 us -> 0 us
  starting transfers between devices: 14.4 us -> 0 us
    dot_general x99 -> x0, matrix products: 85.6 us -> none  [the longest x24 34 us: second_factor(): jnp.dot(rank_proj, up_tile, preferred_element_type=jnp.float32)]
    pallas_call x0 -> x5, Pallas kernels: none -> 84 us  [the longest x1 27.6 us: local(): pl.pallas_call(functools.partial(gather_kernel, helpers, servers), out_sh...]
    dynamic_slice x96 -> x0, local copies, waits for them, and re-layouts: 75.2 us -> none  [local(): lax.scan(first_factor, (start_mixed, start_rank), (left_blocks, down_rank...]
    another operation x2 -> x0, loops' own time: 33.1 us -> none  [the longest x1 16.7 us: local(): lax.scan(second_factor, (start_right, start_low), (right_blocks, up_rank,...]
    all_to_all x2 -> x0, blocking collectives: 28.8 us -> none  [the longest x1 18.7 us: local(): lax.all_to_all(summed_rows.reshape(servers, CAP, positions, width_here),...]
    reshape x100 -> x4, local copies, waits for them, and re-layouts: 33 us -> 5.32 us  [the longest x1 2.17 us: local(): hid = hidden_in.reshape(requests, rows, LANES)]
    all_to_all x3 -> x0, waiting for transfers between devices: 17.7 us -> none  [the longest x1 14.1 us: local(): lax.all_to_all(packed.reshape(servers, CAP, positions, width_here), 'serv...]
    all_to_all x3 -> x0, starting transfers between devices: 14.4 us -> none  [the longest x1 7.39 us: local(): lax.all_to_all(labels.reshape(servers, CAP), 'server', split_axis=0, conc...]
  transfers between devices with their start and end apart: 3 -> 0, of which waited for: 2 -> 0; matrix products, arithmetic and copies ran while one was open for 1% -> 0% of each run, Pallas kernels for 0% -> 0%
where the time goes in v1:
time: 94.8 us; the launch traced here: 93.1 us
  Pallas kernels  84 us (89%)
  local copies, waits for them, and re-layouts  7.52 us (8%)
  other arithmetic  1.49 us (2%)
    pallas_call x1, Pallas kernels, local(): pl.pallas_call(functools.partial(gather_kernel, helpers, servers), out_sh...  27.6 us
    pallas_call x1, Pallas kernels, local(): pl.pallas_call(functools.partial(scatter_kernel, servers), out_shape=(jax...  18.5 us
    pallas_call x1, Pallas kernels, local(): pl.pallas_call(first_kernel, out_shape=(half, thin), grid_spec=pltpu.Pref...  13.2 us
    pallas_call x1, Pallas kernels, local(): pl.pallas_call(functools.partial(swap_kernel, helpers), out_shape=(jax.Sh...  12.7 us
    pallas_call x1, Pallas kernels, local(): pl.pallas_call(second_kernel, out_shape=(half, jax.ShapeDtypeStruct((slot...  12 us
    reshape x1, local copies, waits for them, and re-layouts, local(): hid = hidden_in.reshape(requests, rows, LANES)  2.17 us
    reshape x1, local copies, waits for them, and re-layouts, local(): return out.reshape(requests, positions, width_here)  1.96 us

profile of v1, /device:TPU:0, one launch (start us, length us, event | category | flops | bytes accessed | tf_op | source)
XLA Modules:
  0.0 93.1 jit_solution(10868317079778064673)
XLA Ops:
  0.0 0.7 and_select_fusion
  0.7 0.2 convert_reduce_fusion
  0.9 0.0 copy-start.1
  0.9 0.6 select_reduce_fusion
  1.5 0.1 reshape.21
  1.6 0.6 broadcast_in_dim.32.lab
  2.2 2.2 %reshape.20.hid = bf16[32,64,128]{2,1,0:T(8,128)(2,1)} reshape(bf16[32,4,2048]{2,1,0:T(4,128)(2,1)} %param.7) | data formatting | bytes 1048576 | tf_op jit(solution)/shard_map/reshape | solution.py:426
  4.4 18.5 %scatter.1 = (bf16[16,2,64,128]{3,2,1,0:T(8,128)(2,1)}, s32[16,8,128]{2,1,0:T(8,128)}) custom-call(s32[32]{0:T(128)} %get-tuple-element.22.inv, bf16[32,64,128]{2,1,0:T(8,128)(2,1)} %reshape.20.hid, s32[16,8,128]{2,1,0:T(8,128)} %broadcast_in_dim.32.lab), custom_call_target="tpu_custom_call" | custom-call | tf_op jit(solution)/shard_map/scatter/pallas_call | solution.py:428
  22.9 0.9 slice_reduce_fusion
  23.8 0.7 reshape_squeeze.3.labels
  24.5 13.2 %first.1 = (bf16[2,32,16,256]{3,2,1,0:T(8,128)(2,1)}, f32[32,4,128]{2,1,0:T(4,128)}) custom-call(s32[32]{0:T(128)} %reshape_squeeze.3.labels, bf16[32,64,128]{2,1,0:T(8,128)(2,1)} %bitcast.6, bf16[24,32,4096]{2,1,0:T(8,128)(2,1)} %refs_3_.2, bf16[24,32,4096]{2,1,0:T(8,128)(2,1)} %refs_3_.2, bf16[24,32,4096]{2,1,0:T(8,128)(2,1)} %refs_3_.2, ...), custom_call_target="tpu_custom_call" | custom-call | tf_op jit(solution)/shard_map/first/pallas_call | solution.py:456
  37.7 0.0 copy-done.1
  37.7 12.7 %swap.1 = (bf16[32,256,128]{2,1,0:T(8,128)(2,1)}, f32[32,4,128]{2,1,0:T(4,128)}) custom-call(bf16[2,32,16,256]{3,2,1,0:T(8,128)(2,1)} %get-tuple-element.15.mixed, f32[32,4,128]{2,1,0:T(4,128)} %get-tuple-element.16.rank), custom_call_target="tpu_custom_call" | custom-call | tf_op jit(solution)/shard_map/swap/pallas_call | solution.py:474
  50.4 0.0 copy-start
  50.4 12.0 %second.1 = (bf16[2,32,16,256]{3,2,1,0:T(8,128)(2,1)}, bf16[32,64,128]{2,1,0:T(8,128)(2,1)}) custom-call(s32[32]{0:T(128)} %reshape_squeeze.3.labels, bf16[32,256,128]{2,1,0:T(8,128)(2,1)} %get-tuple-element.17.weights, f32[32,4,128]{2,1,0:T(4,128)} %get-tuple-element.18.proj, bf16[24,32,4096]{2,1,0:T(8,128)(2,1)} %refs_3_.3, bf16[24,32,4096]{2,1,0:T(8,128)(2,1)} %refs_3_.3, ...), custom_call_target="tpu_custom_call" | custom-call | tf_op jit(solution)/shard_map/second/pallas_call | solution.py:487
  62.4 0.0 copy-done
  62.4 1.1 %reshape.23.base = bf16[32,64,128]{2,1,0:T(8,128)(2,1)} reshape(bf16[32,4,2048]{2,1,0:T(4,128)(2,1)S(1)} %copy-done) | data formatting | bytes 1048576 | tf_op jit(solution)/shard_map/reshape | solution.py:514
  63.5 27.6 %gather.1 = bf16[32,64,128]{2,1,0:T(8,128)(2,1)} custom-call(s32[32]{0:T(128)} %copy-done.1, bf16[2,32,16,256]{3,2,1,0:T(8,128)(2,1)} %get-tuple-element.19.right_out, bf16[32,64,128]{2,1,0:T(8,128)(2,1)} %get-tuple-element.20.rank_out, bf16[32,64,128]{2,1,0:T(8,128)(2,1)} %reshape.23.base), custom_call_target="tpu_custom_call" | custom-call | tf_op jit(solution)/shard_map/gather/pallas_call | solution.py:500
  91.1 2.0 %reshape.24 = bf16[32,4,2048]{2,1,0:T(4,128)(2,1)} reshape(bf16[32,64,128]{2,1,0:T(8,128)(2,1)} %gather.1) | data formatting | bytes 1048576 | tf_op jit(solution)/shard_map/reshape | solution.py:515
  (2 shorter events, 0.0 us)
Async XLA Ops:
  0.9 36.9 %copy-start.1 = (s32[32]{0:T(128)}, s32[32]{0:T(128)S(1)}, u32[]{:S(2)}) copy-start(s32[32]{0:T(128)S(1)} %multiply_add_fusion.tgt) | copy-start | bytes 388
  50.4 12.0 %copy-start = (bf16[32,4,2048]{2,1,0:T(4,128)(2,1)S(1)}, bf16[32,4,2048]{2,1,0:T(4,128)(2,1)}, u32[]{:S(2)}) copy-start(bf16[32,4,2048]{2,1,0:T(4,128)(2,1)} %param.8) | copy-start | bytes 1572868

commit v2 on v0

--- a/solution.py
+++ b/solution.py
@@ -1,13 +1,17 @@
+import functools
+
 import jax
 import jax.numpy as jnp
 from jax import lax
+from jax.experimental import pallas as pl
+from jax.experimental.pallas import tpu as pltpu
 from jax.sharding import PartitionSpec as P
 
 BLOCK = 64
 CAP = 2
 
 
-def local(hidden_in, base_out, adapter_ids, left_blocks, right_blocks, down_rank, up_rank):
+def plain(hidden_in, base_out, adapter_ids, left_blocks, right_blocks, down_rank, up_rank):
     servers = lax.axis_size("server")
     requests, positions, width_here = hidden_in.shape
     adapters_here = left_blocks.shape[0]
@@ -114,6 +118,395 @@
     return total.astype(jnp.bfloat16)
 
 
+LANES = 128
+CHUNKS = 4
+MESH = pl.DeviceIdType.MESH
+NT = (((1,), (1,)), ((), ()))
+BF = jnp.bfloat16
+F32 = jnp.float32
+
+
+def lanes_of(shape, dim=1):
+    return lax.broadcasted_iota(jnp.int32, shape, dim)
+
+
+def flipped(index, mask):
+    other = index
+    bit = 1
+    while bit <= mask:
+        if mask & bit:
+            other = other + bit * (1 - 2 * (lax.rem(lax.div(index, bit), 2)))
+        bit *= 2
+    return other
+
+
+def stacked(ref, at, width):
+    return jnp.concatenate(
+        [ref[at, :, k * LANES : (k + 1) * LANES] for k in range(width // LANES)], axis=0
+    )
+
+
+def fused_kernel(
+    helpers, count,
+    inv, tgt, hid, lab, base, left_any, right_any, down_any, up_any,
+    out,
+    left, right, down, up, packed, arrived, lab_in, lab_s,
+    mixed, got1, rank, got_rank, weights, proj, right_out, got2, low, delta, back,
+    pick1, pick2,
+    wsem, send, recv, lsend, lrecv, lsem, s1, r1, s2, r2, s3, r3, bsend, brecv,
+):
+    me = lax.axis_index("helper")
+    here = lax.axis_index("server")
+    slots, rows, _ = packed.shape
+    rows_out, wide = mixed.shape[2:]
+    blocks, flat = left.shape[1:]
+    rank_width = down.shape[1]
+    positions = rank.shape[1]
+    tiles = rows // positions
+    cap = slots // count
+    steps = count // CHUNKS
+    size = slots // CHUNKS
+    half = wide // 2
+    loads = [
+        pltpu.make_async_copy(a, b, wsem.at[i])
+        for i, (a, b) in enumerate(
+            ((left_any, left), (down_any, down), (right_any, right), (up_any, up))
+        )
+    ]
+    for load in loads:
+        load.start()
+    barrier = pltpu.get_barrier_semaphore()
+    for step in range(1, count):
+        pl.semaphore_signal(
+            barrier, inc=1, device_id={"server": flipped(here, step)}, device_id_type=MESH
+        )
+    for step in range(1, helpers):
+        peer = lax.rem(me + step, helpers)
+        pl.semaphore_signal(barrier, inc=1, device_id={"helper": peer}, device_id_type=MESH)
+    for s in range(slots):
+        packed[s] = hid[inv[s]]
+    pl.semaphore_wait(barrier, helpers + count - 2)
+    order = list(range(1, CHUNKS)) + [0]
+    waits = [[] for _ in range(CHUNKS)]
+    sent = []
+    for c in order:
+        for step in range(c * steps, (c + 1) * steps):
+            at = pl.ds(step * cap, cap)
+            if step == 0:
+                arrived[at] = packed[at]
+                lab_in[0] = lab[0]
+                continue
+            peer = flipped(here, step)
+            for src, dst, s, r in (
+                (lab.at[step], lab_in.at[step], lsend, lrecv),
+                (packed.at[at], arrived.at[at], send, recv),
+            ):
+                copy = pltpu.make_async_remote_copy(
+                    src_ref=src, dst_ref=dst, send_sem=s.at[step], recv_sem=r.at[step],
+                    device_id={"server": peer}, device_id_type=MESH,
+                )
+                copy.start()
+                waits[c].append(copy)
+
+    src = lanes_of((wide, wide), 0)
+    dst = lanes_of((wide, wide))
+    block = 2 * (src % tiles) + (src // (half // 2)) % 2
+    for h in range(helpers):
+        pick1[h] = (
+            (dst // LANES == (dst // (LANES // 2)) % 2)
+            & (dst % (LANES // 2) == 2 * tiles * h + block)
+        ).astype(F32).astype(BF)
+    src = lanes_of((wide, LANES), 0)
+    dst = lanes_of((wide, LANES))
+    number = 2 * (src % rows_out) + (src // (rows_out * positions)) % 2
+    for h in range(helpers):
+        pick2[h] = (
+            (src // (2 * rows_out * positions) == dst // (LANES // 2))
+            & (dst % (LANES // 2) == 2 * rows_out * h + number)
+        ).astype(F32).astype(BF)
+    few = lanes_of((rows, LANES)) < LANES // 2
+    lane = lanes_of((blocks, wide))
+    row = lanes_of((blocks, wide), 0)
+    keep1 = row == 2 * (lane % tiles) + (lane // rows) % 2
+    keep2 = row == 2 * (lane % rows_out) + (lane // (rows_out * positions)) % 2
+    same = lanes_of((rows, wide), 0) % tiles == lanes_of((rows, wide)) // rank_width
+    fold = (
+        lanes_of((wide, LANES), 0) % rank_width == lanes_of((wide, LANES)) % rank_width
+    ).astype(F32).astype(BF)
+    one = lanes_of((1, wide))
+    code1 = (one // half) * positions + (one // tiles) % positions
+    code2 = (one // rows_out) % positions
+
+    def to_helpers(chunk, pairs):
+        at = pl.ds(chunk * size, size)
+        copies = []
+        for step in range(1, helpers):
+            peer = lax.rem(me + step, helpers)
+            for src_ref, dst_ref, s, r, split in pairs:
+                copy = pltpu.make_async_remote_copy(
+                    src_ref=src_ref.at[peer, at] if split else src_ref.at[at],
+                    dst_ref=dst_ref.at[me, at],
+                    send_sem=s.at[chunk, step],
+                    recv_sem=r.at[chunk, step],
+                    device_id={"helper": peer},
+                    device_id_type=MESH,
+                )
+                copy.start()
+                copies.append(copy)
+        for src_ref, dst_ref, s, r, split in pairs:
+            dst_ref[me, at] = src_ref[me, at] if split else src_ref[at]
+        return copies
+
+    def first(chunk):
+        for copy in waits[chunk]:
+            copy.wait_recv()
+        sent.extend(waits[chunk])
+        k = pl.ds(chunk * steps, steps)
+        copy = pltpu.make_async_copy(lab_in.at[k], lab_s.at[k], lsem.at[chunk])
+        copy.start()
+        copy.wait()
+
+        def body(i, carry):
+            for u in range(cap):
+                slot = chunk * size + i * cap + u
+                which = lab_s[chunk * steps + i, 0, u]
+                x = arrived[slot]
+                xf = x.astype(F32)
+                turned = pltpu.roll(xf, LANES // 2, 1)
+                zero = jnp.zeros_like(xf)
+                fixed = jnp.concatenate(
+                    [
+                        jnp.where(few, xf, zero),
+                        jnp.where(few, turned, zero),
+                        jnp.where(few, zero, turned),
+                        jnp.where(few, zero, xf),
+                    ],
+                    axis=0,
+                ).astype(BF)
+                full = lax.dot_general(
+                    stacked(left, which, flat), fixed, NT, preferred_element_type=F32
+                ).reshape(flat // LANES, blocks, wide)
+                got = jnp.sum(jnp.where(keep1[None], full, 0.0), axis=1).astype(BF)
+                for h in range(helpers):
+                    mixed[h, slot] = got[h * rows_out : (h + 1) * rows_out]
+                part = lax.dot_general(
+                    x, stacked(down, which, tiles * LANES), NT, preferred_element_type=F32
+                )
+                part = jnp.where(same, part, 0.0).reshape(positions, tiles, wide)
+                part = jnp.sum(part, axis=1)
+                high = part.astype(BF)
+                rest = (part - high.astype(F32)).astype(BF)
+                rank[slot] = jnp.dot(high, fold, preferred_element_type=F32) + jnp.dot(
+                    rest, fold, preferred_element_type=F32
+                )
+            return carry
+
+        lax.fori_loop(0, steps, body, 0)
+        return to_helpers(chunk, ((mixed, got1, s1, r1, True), (rank, got_rank, s2, r2, False)))
+
+    def second(chunk, copies):
+        for copy in copies:
+            copy.wait()
+        at = pl.ds(chunk * size, size)
+        total = got_rank[0, at]
+        for h in range(1, helpers):
+            total = total + got_rank[h, at]
+        proj[at] = total.astype(BF).astype(F32)
+        acc = None
+        for h in range(helpers):
+            flat_rows = got1[h, at].reshape(size * rows_out, wide)
+            tall = jnp.concatenate(
+                [
+                    flat_rows * (code1 == q).astype(F32).astype(BF)
+                    for q in range(2 * positions)
+                ],
+                axis=0,
+            )
+            term = jnp.dot(tall, pick1[h], preferred_element_type=F32)
+            acc = term if acc is None else acc + term
+        acc = acc.astype(BF)
+        span = size * rows_out
+        for q in range(2 * positions):
+            for c in range(2):
+                to = (c * 2 * positions + q) * rows_out
+                weights[at, to : to + rows_out, :] = acc[
+                    q * span : (q + 1) * span, c * LANES : (c + 1) * LANES
+                ].reshape(size, rows_out, LANES)
+
+        def body(i, carry):
+            for u in range(cap):
+                slot = chunk * size + i * cap + u
+                which = lab_s[chunk * steps + i, 0, u]
+                full = lax.dot_general(
+                    stacked(right, which, flat), weights[slot], NT, preferred_element_type=F32
+                ).reshape(flat // LANES, blocks, wide)
+                got = jnp.sum(jnp.where(keep2[None], full, 0.0), axis=1).astype(BF)
+                for h in range(helpers):
+                    right_out[h, slot] = got[h * rows_out : (h + 1) * rows_out]
+                p = proj[slot]
+                tall = jnp.concatenate(
+                    [jnp.broadcast_to(p[j : j + 1], (tiles, LANES)) for j in range(positions)],
+                    axis=0,
+                )
+                tall = jnp.concatenate([tall] * (wide // LANES), axis=1)
+                tall = jnp.where(same, tall, 0.0).astype(BF)
+                low[slot] = jnp.dot(
+                    tall, stacked(up, which, tiles * LANES), preferred_element_type=F32
+                ).astype(BF)
+            return carry
+
+        lax.fori_loop(0, steps, body, 0)
+        return to_helpers(chunk, ((right_out, got2, s3, r3, True),))
+
+    def third(chunk, copies):
+        for copy in copies:
+            copy.wait()
+        at = pl.ds(chunk * size, size)
+        acc = None
+        for h in range(helpers):
+            flat_rows = got2[h, at].reshape(size * rows_out, wide)
+            tall = jnp.concatenate(
+                [flat_rows * (code2 == p).astype(F32).astype(BF) for p in range(positions)],
+                axis=0,
+            )
+            term = jnp.dot(tall, pick2[h], preferred_element_type=F32)
+            acc = term if acc is None else acc + term
+        span = size * rows_out
+        for p in range(positions):
+            r = slice(p * rows_out, (p + 1) * rows_out)
+            more = low[at, r, :].reshape(span, LANES).astype(F32)
+            delta[at, r, :] = (
+                (acc[p * span : (p + 1) * span] + more).astype(BF).reshape(size, rows_out, LANES)
+            )
+        result = []
+        for step in range(chunk * steps, (chunk + 1) * steps):
+            place = pl.ds(step * cap, cap)
+            if step == 0:
+                back[place] = delta[place]
+                continue
+            copy = pltpu.make_async_remote_copy(
+                src_ref=delta.at[place], dst_ref=back.at[place],
+                send_sem=bsend.at[step], recv_sem=brecv.at[step],
+                device_id={"server": flipped(here, step)}, device_id_type=MESH,
+            )
+            copy.start()
+            result.append(copy)
+        return result
+
+    loads[0].wait()
+    loads[1].wait()
+    one_done, two_done, final = {}, {}, []
+    for i in range(CHUNKS + 2):
+        if i < CHUNKS:
+            one_done[i] = first(order[i])
+        if i == 0:
+            loads[2].wait()
+            loads[3].wait()
+        if 1 <= i <= CHUNKS:
+            two_done[i - 1] = second(order[i - 1], one_done[i - 1])
+        if i >= 2:
+            final += third(order[i - 2], two_done[i - 2])
+    for copy in sent:
+        copy.wait_send()
+    for copy in final:
+        copy.wait()
+    for r in range(out.shape[0]):
+        out[r] = (base[r].astype(F32) + back[tgt[r]].astype(F32)).astype(BF)
+
+
+VM = pl.BlockSpec(memory_space=pltpu.VMEM)
+SM = pl.BlockSpec(memory_space=pltpu.SMEM)
+ANY = pl.BlockSpec(memory_space=pl.ANY)
+
+
+def local(hidden_in, base_out, adapter_ids, left_blocks, right_blocks, down_rank, up_rank):
+    servers = lax.axis_size("server")
+    helpers = lax.axis_size("helper")
+    requests, positions, width_here = hidden_in.shape
+    adapters_here, blocks_here, flat = left_blocks.shape
+    rank_width = down_rank.shape[2]
+    tiles = width_here // LANES
+    rows = positions * tiles
+    wide = 4 * rows
+    slots = servers * CAP
+    rows_out = flat // LANES // helpers
+    fits = (
+        2 * tiles == blocks_here
+        and rows_out == tiles
+        and wide == 2 * LANES
+        and tiles * rank_width == wide
+        and tiles % 16 == 0
+        and servers & (servers - 1) == 0
+        and servers % CHUNKS == 0
+        and 2 * helpers * tiles == BLOCK
+    )
+    if not fits:
+        return plain(
+            hidden_in, base_out, adapter_ids, left_blocks, right_blocks, down_rank, up_rank
+        )
+    owners = adapter_ids // adapters_here
+    local_id = adapter_ids % adapters_here
+    number = jnp.arange(requests, dtype=jnp.int32)
+    earlier = (owners[:, None] == owners[None, :]) & (number[None, :] < number[:, None])
+    step = owners ^ lax.axis_index("server")
+    target = step * CAP + jnp.sum(earlier.astype(jnp.int32), axis=1)
+    hit = jnp.arange(slots, dtype=jnp.int32)[:, None] == target[None, :]
+    inv = jnp.sum(jnp.where(hit, number[None, :], 0), axis=1)
+    labels = jnp.sum(jnp.where(hit, local_id[None, :], 0), axis=1)
+    lab = jnp.pad(labels.reshape(servers, 1, CAP), ((0, 0), (0, 0), (0, LANES - CAP)))
+    dma = pltpu.SemaphoreType.DMA
+    by_slot = pltpu.VMEM((slots, rows, LANES), BF)
+    split = pltpu.VMEM((helpers, slots, rows_out, wide), BF)
+    down = jnp.swapaxes(down_rank, 1, 2)
+    out = pl.pallas_call(
+        functools.partial(fused_kernel, helpers, servers),
+        out_shape=jax.ShapeDtypeStruct((requests, rows, LANES), BF),
+        in_specs=[SM, SM, VM, VM, VM, ANY, ANY, ANY, ANY],
+        out_specs=VM,
+        scratch_shapes=[
+            pltpu.VMEM(left_blocks.shape, BF),
+            pltpu.VMEM(right_blocks.shape, BF),
+            pltpu.VMEM(down.shape, BF),
+            pltpu.VMEM(up_rank.shape, BF),
+            by_slot,
+            by_slot,
+            pltpu.VMEM(lab.shape, jnp.int32),
+            pltpu.SMEM(lab.shape, jnp.int32),
+            split,
+            split,
+            pltpu.VMEM((slots, positions, LANES), F32),
+            pltpu.VMEM((helpers, slots, positions, LANES), F32),
+            pltpu.VMEM((slots, wide, LANES), BF),
+            pltpu.VMEM((slots, positions, LANES), F32),
+            split,
+            split,
+            by_slot,
+            by_slot,
+            by_slot,
+            pltpu.VMEM((helpers, wide, wide), BF),
+            pltpu.VMEM((helpers, wide, LANES), BF),
+            dma((4,)),
+        ]
+        + [dma((servers,))] * 4
+        + [dma((CHUNKS,))]
+        + [dma((CHUNKS, helpers))] * 6
+        + [dma((servers,))] * 2,
+        compiler_params=pltpu.CompilerParams(collective_id=0, has_side_effects=True),
+        name="fused",
+    )(
+        inv,
+        target,
+        hidden_in.reshape(requests, rows, LANES),
+        lab,
+        base_out.reshape(requests, rows, LANES),
+        left_blocks,
+        right_blocks,
+        down,
+        up_rank,
+    )
+    return out.reshape(requests, positions, width_here)
+
+
 def solution(mesh):
     in_specs = (
         P("server", None, "helper"),

time: 314 us -> 57.4 us (0.18); the launches traced: 310 us -> 57.1 us
  local copies, waits for them, and re-layouts: 118 us -> 6.98 us
  matrix products: 85.6 us -> 0 us
  Pallas kernels: 0 us -> 48.6 us
  blocking collectives: 37.5 us -> 0 us
  loops' own time: 33.1 us -> 0 us
  waiting for transfers between devices: 17.7 us -> 0 us
  starting transfers between devices: 14.4 us -> 0 us
    dot_general x99 -> x0, matrix products: 85.6 us -> none  [the longest x24 34 us: second_factor(): jnp.dot(rank_proj, up_tile, preferred_element_type=jnp.float32)]
    dynamic_slice x96 -> x0, local copies, waits for them, and re-layouts: 75.2 us -> none  [local(): lax.scan(first_factor, (start_mixed, start_rank), (left_blocks, down_rank...]
    pallas_call x0 -> x1, Pallas kernels: none -> 48.6 us  [local(): pl.pallas_call(functools.partial(fused_kernel, helpers, servers), out_sha...]
    another operation x2 -> x0, loops' own time: 33.1 us -> none  [the longest x1 16.7 us: local(): lax.scan(second_factor, (start_right, start_low), (right_blocks, up_rank,...]
    all_to_all x2 -> x0, blocking collectives: 28.8 us -> none  [the longest x1 18.7 us: local(): lax.all_to_all(summed_rows.reshape(servers, CAP, positions, width_here),...]
    reshape x100 -> x4, local copies, waits for them, and re-layouts: 33 us -> 6.36 us  [the longest x1 2.17 us: local(): hidden_in.reshape(requests, rows, LANES)]
    all_to_all x3 -> x0, waiting for transfers between devices: 17.7 us -> none  [the longest x1 14.1 us: local(): lax.all_to_all(packed.reshape(servers, CAP, positions, width_here), 'serv...]
    all_to_all x3 -> x0, starting transfers between devices: 14.4 us -> none  [the longest x1 7.39 us: local(): lax.all_to_all(labels.reshape(servers, CAP), 'server', split_axis=0, conc...]
  transfers between devices with their start and end apart: 3 -> 0, of which waited for: 2 -> 0; matrix products, arithmetic and copies ran while one was open for 1% -> 0% of each run, Pallas kernels for 0% -> 0%
where the time goes in v2:
time: 57.4 us; the launch traced here: 57.1 us
  Pallas kernels  48.6 us (85%)
  local copies, waits for them, and re-layouts  6.98 us (12%)
  other arithmetic  1.48 us (3%)
    pallas_call x1, Pallas kernels, local(): pl.pallas_call(functools.partial(fused_kernel, helpers, servers), out_sha...  48.6 us
    reshape x1, local copies, waits for them, and re-layouts, local(): hidden_in.reshape(requests, rows, LANES)  2.17 us
    reshape x1, local copies, waits for them, and re-layouts, local(): base_out.reshape(requests, rows, LANES)  2.16 us
    reshape x1, local copies, waits for them, and re-layouts, local(): return out.reshape(requests, positions, width_here)  1.96 us

profile of v2, /device:TPU:0, one launch (start us, length us, event | category | flops | bytes accessed | tf_op | source)
XLA Modules:
  0.0 57.1 jit_solution(12082617563364962100)
XLA Ops:
  0.0 0.7 %and_select_fusion.1 = (s32[32]{0:T(128)S(1)}, s32[32]{0:T(128)S(1)}) fusion(s32[32]{0:T(128)} %param.9), kind=kLoop, calls=%fused_computation.7 | loop fusion | flops 384 | bytes 384 | tf_op jit(solution)/shard_map/jit(floor_divide)/jit(_where)/select_n | solution.py:447
  0.7 0.2 convert_reduce_fusion
  0.9 0.0 copy-start
  0.9 0.6 %select_reduce_fusion = (s32[32]{0:T(128)S(1)}, s32[32]{0:T(128)}) fusion(s32[32]{0:T(128)S(1)} %get-tuple-element.8, s32[32]{0:T(128)S(1)} %multiply_add_fusion.tgt), kind=kLoop, calls=%fused_computation | loop fusion | flops 5056 | bytes 512 | tf_op jit(solution)/shard_map/reduce_sum | solution.py:455
  1.5 0.1 reshape.17
  1.6 0.6 %pad.4.lab = s32[16,1,128]{2,1,0:T(1,128)} pad(s32[16,1,2]{2,1,0:T(1,128)S(1)} %bitcast.3, s32[]{:T(128)} %constant.24.clone.1), padding=0_0x0_0x0_126 | pad | bytes 8324 | tf_op jit(solution)/shard_map/jit(_pad)/pad | solution.py:456
  2.2 2.2 %reshape.16.hid = bf16[32,64,128]{2,1,0:T(8,128)(2,1)} reshape(bf16[32,4,2048]{2,1,0:T(4,128)(2,1)} %param.7) | data formatting | bytes 1048576 | tf_op jit(solution)/shard_map/reshape | solution.py:499
  4.4 2.2 %reshape.18.base = bf16[32,64,128]{2,1,0:T(8,128)(2,1)} reshape(bf16[32,4,2048]{2,1,0:T(4,128)(2,1)} %param.8) | data formatting | bytes 1048576 | tf_op jit(solution)/shard_map/reshape | solution.py:501
  6.5 0.0 copy-done
  6.5 48.6 %fused.1 = bf16[32,64,128]{2,1,0:T(8,128)(2,1)} custom-call(s32[32]{0:T(128)} %get-tuple-element.6.inv, s32[32]{0:T(128)} %copy-done, bf16[32,64,128]{2,1,0:T(8,128)(2,1)} %reshape.16.hid, s32[16,1,128]{2,1,0:T(1,128)} %pad.4.lab, bf16[32,64,128]{2,1,0:T(8,128)(2,1)} %reshape.18.base, bf16[24,32,4096]{2,1,0:T(8,128)(2,1)} %left_any.1, ...), custom_call_target="tpu_custom_call" | custom-call | tf_op jit(solution)/shard_map/fused/pallas_call | solution.py:461
  55.2 2.0 %reshape.19 = bf16[32,4,2048]{2,1,0:T(4,128)(2,1)} reshape(bf16[32,64,128]{2,1,0:T(8,128)(2,1)} %fused.1) | data formatting | bytes 1048576 | tf_op jit(solution)/shard_map/reshape | solution.py:507
  (1 shorter events, 0.0 us)
Async XLA Ops:
  0.9 5.7 %copy-start = (s32[32]{0:T(128)}, s32[32]{0:T(128)S(1)}, u32[]{:S(2)}) copy-start(s32[32]{0:T(128)S(1)} %multiply_add_fusion.tgt) | copy-start | bytes 388

commit v3 on v2

--- a/solution.py
+++ b/solution.py
@@ -184,7 +184,7 @@
         peer = lax.rem(me + step, helpers)
         pl.semaphore_signal(barrier, inc=1, device_id={"helper": peer}, device_id_type=MESH)
     for s in range(slots):
-        packed[s] = hid[inv[s]]
+        packed[s] = hid[inv[s]].astype(F32).reshape(rows, LANES).astype(BF)
     pl.semaphore_wait(barrier, helpers + count - 2)
     order = list(range(1, CHUNKS)) + [0]
     waits = [[] for _ in range(CHUNKS)]
@@ -210,7 +210,7 @@
 
     src = lanes_of((wide, wide), 0)
     dst = lanes_of((wide, wide))
-    block = 2 * (src % tiles) + (src // (half // 2)) % 2
+    block = 2 * ((src // positions) % tiles) + (src // rows) % 2
     for h in range(helpers):
         pick1[h] = (
             (dst // LANES == (dst // (LANES // 2)) % 2)
@@ -225,17 +225,22 @@
             & (dst % (LANES // 2) == 2 * rows_out * h + number)
         ).astype(F32).astype(BF)
     few = lanes_of((rows, LANES)) < LANES // 2
+    row_of = lanes_of((rows, rows), 0)
     lane = lanes_of((blocks, wide))
     row = lanes_of((blocks, wide), 0)
-    keep1 = row == 2 * (lane % tiles) + (lane // rows) % 2
+    keep1 = row == 2 * ((lane // positions) % tiles) + (lane // rows) % 2
     keep2 = row == 2 * (lane % rows_out) + (lane // (rows_out * positions)) % 2
-    same = lanes_of((rows, wide), 0) % tiles == lanes_of((rows, wide)) // rank_width
+    same = lanes_of((rows, wide), 0) // positions == lanes_of((rows, wide)) // rank_width
     fold = (
         lanes_of((wide, LANES), 0) % rank_width == lanes_of((wide, LANES)) % rank_width
     ).astype(F32).astype(BF)
     one = lanes_of((1, wide))
-    code1 = (one // half) * positions + (one // tiles) % positions
+    code1 = (one // half) * positions + one % positions
     code2 = (one // rows_out) % positions
+
+    turn = (
+        lanes_of((rows, rows)) == (row_of % positions) * tiles + row_of // positions
+    ).astype(F32).astype(BF)
 
     def to_helpers(chunk, pairs):
         at = pl.ds(chunk * size, size)
@@ -292,8 +297,9 @@
                 part = lax.dot_general(
                     x, stacked(down, which, tiles * LANES), NT, preferred_element_type=F32
                 )
-                part = jnp.where(same, part, 0.0).reshape(positions, tiles, wide)
-                part = jnp.sum(part, axis=1)
+                part = jnp.where(same, part, 0.0).reshape(rows // 8, 8, wide)
+                part = jnp.sum(part, axis=0)
+                part = sum(part[j : j + positions] for j in range(0, 8, positions))
                 high = part.astype(BF)
                 rest = (part - high.astype(F32)).astype(BF)
                 rank[slot] = jnp.dot(high, fold, preferred_element_type=F32) + jnp.dot(
@@ -344,10 +350,7 @@
                 for h in range(helpers):
                     right_out[h, slot] = got[h * rows_out : (h + 1) * rows_out]
                 p = proj[slot]
-                tall = jnp.concatenate(
-                    [jnp.broadcast_to(p[j : j + 1], (tiles, LANES)) for j in range(positions)],
-                    axis=0,
-                )
+                tall = jnp.concatenate([p] * tiles, axis=0)
                 tall = jnp.concatenate([tall] * (wide // LANES), axis=1)
                 tall = jnp.where(same, tall, 0.0).astype(BF)
                 low[slot] = jnp.dot(
@@ -372,12 +375,17 @@
             term = jnp.dot(tall, pick2[h], preferred_element_type=F32)
             acc = term if acc is None else acc + term
         span = size * rows_out
-        for p in range(positions):
-            r = slice(p * rows_out, (p + 1) * rows_out)
-            more = low[at, r, :].reshape(span, LANES).astype(F32)
-            delta[at, r, :] = (
-                (acc[p * span : (p + 1) * span] + more).astype(BF).reshape(size, rows_out, LANES)
-            )
+        for i in range(size):
+            mine = jnp.concatenate(
+                [
+                    acc[p * span + i * rows_out : p * span + (i + 1) * rows_out]
+                    for p in range(positions)
+                ],
+                axis=0,
+            ).astype(BF)
+            mine = jnp.dot(turn, mine, preferred_element_type=F32)
+            slot = chunk * size + i
+            delta[slot] = (mine + low[slot].astype(F32)).astype(BF)
         result = []
         for step in range(chunk * steps, (chunk + 1) * steps):
             place = pl.ds(step * cap, cap)
@@ -411,7 +419,8 @@
     for copy in final:
         copy.wait()
     for r in range(out.shape[0]):
-        out[r] = (base[r].astype(F32) + back[tgt[r]].astype(F32)).astype(BF)
+        added = back[tgt[r]].astype(F32).reshape(tiles, positions, LANES)
+        out[r] = (base[r].astype(F32) + added).astype(BF)
 
 
 VM = pl.BlockSpec(memory_space=pltpu.VMEM)
@@ -439,6 +448,7 @@
         and servers & (servers - 1) == 0
         and servers % CHUNKS == 0
         and 2 * helpers * tiles == BLOCK
+        and 8 % positions == 0
     )
     if not fits:
         return plain(
@@ -454,13 +464,18 @@
     inv = jnp.sum(jnp.where(hit, number[None, :], 0), axis=1)
     labels = jnp.sum(jnp.where(hit, local_id[None, :], 0), axis=1)
     lab = jnp.pad(labels.reshape(servers, 1, CAP), ((0, 0), (0, 0), (0, LANES - CAP)))
+
+    def tiled(array):
+        split_rows = array.reshape(requests, positions, tiles, LANES)
+        return split_rows.transpose(0, 2, 1, 3)
+
     dma = pltpu.SemaphoreType.DMA
     by_slot = pltpu.VMEM((slots, rows, LANES), BF)
     split = pltpu.VMEM((helpers, slots, rows_out, wide), BF)
     down = jnp.swapaxes(down_rank, 1, 2)
     out = pl.pallas_call(
         functools.partial(fused_kernel, helpers, servers),
-        out_shape=jax.ShapeDtypeStruct((requests, rows, LANES), BF),
+        out_shape=jax.ShapeDtypeStruct((requests, tiles, positions, LANES), BF),
         in_specs=[SM, SM, VM, VM, VM, ANY, ANY, ANY, ANY],
         out_specs=VM,
         scratch_shapes=[
@@ -496,15 +511,15 @@
     )(
         inv,
         target,
-        hidden_in.reshape(requests, rows, LANES),
+        tiled(hidden_in),
         lab,
-        base_out.reshape(requests, rows, LANES),
+        tiled(base_out),
         left_blocks,
         right_blocks,
         down,
         up_rank,
     )
-    return out.reshape(requests, positions, width_here)
+    return out.transpose(0, 2, 1, 3).reshape(requests, positions, width_here)
 
 
 def solution(mesh):

time: 57.4 us -> 53.7 us (0.936)
  local copies, waits for them, and re-layouts: 6.98 us -> 2.76 us
  Pallas kernels: 48.6 us -> 49.2 us
    reshape x3 -> x0, local copies, waits for them, and re-layouts: 6.29 us -> none  [the longest x1 2.17 us: local(): hidden_in.reshape(requests, rows, LANES)]
    unnamed x2 -> x3, local copies, waits for them, and re-layouts: 0.01 us -> 2.06 us
where the time goes in v3:
time: 53.7 us; the launch traced here: 53.5 us
  Pallas kernels  49.2 us (92%)
  local copies, waits for them, and re-layouts  2.76 us (5%)
  other arithmetic  1.56 us (3%)
    pallas_call x1, Pallas kernels, local(): pl.pallas_call(functools.partial(fused_kernel, helpers, servers), out_sha...  49.2 us
    unnamed x3, local copies, waits for them, and re-layouts  2.06 us

profile of v3, /device:TPU:0, one launch (start us, length us, event | category | flops | bytes accessed | tf_op | source)
XLA Modules:
  0.0 53.5 jit_solution(1295554044931573403)
XLA Ops:
  0.0 0.7 %and_select_fusion.1 = (s32[32]{0:T(128)S(1)}, s32[32]{0:T(128)S(1)}) fusion(s32[32]{0:T(128)} %param.9), kind=kLoop, calls=%fused_computation.7 | loop fusion | flops 384 | bytes 384 | tf_op jit(solution)/shard_map/jit(floor_divide)/jit(_where)/select_n | solution.py:457
  0.7 0.2 convert_reduce_fusion
  0.9 0.0 copy-start
  0.9 0.7 %select_reduce_fusion = (s32[32]{0:T(128)S(1)}, s32[32]{0:T(128)}) fusion(s32[32]{0:T(128)S(1)} %get-tuple-element.8, s32[32]{0:T(128)S(1)} %multiply_add_fusion.tgt), kind=kLoop, calls=%fused_computation | loop fusion | flops 5056 | bytes 512 | tf_op jit(solution)/shard_map/reduce_sum | solution.py:465
  1.6 0.1 reshape.17
  1.7 0.6 %pad.4.lab = s32[16,1,128]{2,1,0:T(1,128)} pad(s32[16,1,2]{2,1,0:T(1,128)S(1)} %bitcast.15, s32[]{:T(128)} %constant.24.clone.1), padding=0_0x0_0x0_126 | pad | bytes 8324 | tf_op jit(solution)/shard_map/jit(_pad)/pad | solution.py:466
  2.3 0.0 copy-done
  2.3 49.2 %fused.1 = bf16[32,16,4,128]{3,2,1,0:T(4,128)(2,1)} custom-call(s32[32]{0:T(128)} %get-tuple-element.6.inv, s32[32]{0:T(128)} %copy-done, bf16[32,16,4,128]{3,2,1,0:T(4,128)(2,1)} %bitcast.13, s32[16,1,128]{2,1,0:T(1,128)} %pad.4.lab, bf16[32,16,4,128]{3,2,1,0:T(4,128)(2,1)} %bitcast.14, bf16[24,32,4096]{2,1,0:T(8,128)(2,1)} %left_any.1, ...), custom_call_target="tpu_custom_call" | custom-call | tf_op jit(solution)/shard_map/fused/pallas_call | solution.py:476
  51.5 2.1 %copy.12 = bf16[32,4,2048]{2,1,0:T(4,128)(2,1)} copy(bf16[32,4,2048]{2,1,0:T(4,128)(2,1)} %bitcast.11) | data formatting | bytes 1048576
  (1 shorter events, 0.0 us)
Async XLA Ops:
  0.9 1.4 %copy-start = (s32[32]{0:T(128)}, s32[32]{0:T(128)S(1)}, u32[]{:S(2)}) copy-start(s32[32]{0:T(128)S(1)} %multiply_add_fusion.tgt) | copy-start | bytes 388

commit v4 on v3

--- a/solution.py
+++ b/solution.py
@@ -312,7 +312,8 @@
 
     def second(chunk, copies):
         for copy in copies:
-            copy.wait()
+            copy.wait_recv()
+        sent.extend(copies)
         at = pl.ds(chunk * size, size)
         total = got_rank[0, at]
         for h in range(1, helpers):
@@ -363,7 +364,8 @@
 
     def third(chunk, copies):
         for copy in copies:
-            copy.wait()
+            copy.wait_recv()
+        sent.extend(copies)
         at = pl.ds(chunk * size, size)
         acc = None
         for h in range(helpers):

time: 53.7 us -> 53.7 us (level)
  no operation moved by 1% of the time
where the time goes in v4:
time: 53.7 us; the launch traced here: 53.5 us
  Pallas kernels  49.2 us (92%)
  local copies, waits for them, and re-layouts  2.76 us (5%)
  other arithmetic  1.56 us (3%)
    pallas_call x1, Pallas kernels, local(): pl.pallas_call(functools.partial(fused_kernel, helpers, servers), out_sha...  49.2 us
    unnamed x3, local copies, waits for them, and re-layouts  2.06 us

profile of v4, /device:TPU:0, one launch (start us, length us, event | category | flops | bytes accessed | tf_op | source)
XLA Modules:
  0.0 53.5 jit_solution(5011728265820913735)
XLA Ops:
  0.0 0.7 %and_select_fusion.1 = (s32[32]{0:T(128)S(1)}, s32[32]{0:T(128)S(1)}) fusion(s32[32]{0:T(128)} %param.9), kind=kLoop, calls=%fused_computation.7 | loop fusion | flops 384 | bytes 384 | tf_op jit(solution)/shard_map/jit(floor_divide)/jit(_where)/select_n | solution.py:459
  0.7 0.2 convert_reduce_fusion
  0.9 0.0 copy-start
  0.9 0.7 %select_reduce_fusion = (s32[32]{0:T(128)S(1)}, s32[32]{0:T(128)}) fusion(s32[32]{0:T(128)S(1)} %get-tuple-element.8, s32[32]{0:T(128)S(1)} %multiply_add_fusion.tgt), kind=kLoop, calls=%fused_computation | loop fusion | flops 5056 | bytes 512 | tf_op jit(solution)/shard_map/reduce_sum | solution.py:467
  1.6 0.1 reshape.17
  1.7 0.6 %pad.4.lab = s32[16,1,128]{2,1,0:T(1,128)} pad(s32[16,1,2]{2,1,0:T(1,128)S(1)} %bitcast.15, s32[]{:T(128)} %constant.24.clone.1), padding=0_0x0_0x0_126 | pad | bytes 8324 | tf_op jit(solution)/shard_map/jit(_pad)/pad | solution.py:468
  2.3 0.0 copy-done
  2.3 49.2 %fused.1 = bf16[32,16,4,128]{3,2,1,0:T(4,128)(2,1)} custom-call(s32[32]{0:T(128)} %get-tuple-element.6.inv, s32[32]{0:T(128)} %copy-done, bf16[32,16,4,128]{3,2,1,0:T(4,128)(2,1)} %bitcast.13, s32[16,1,128]{2,1,0:T(1,128)} %pad.4.lab, bf16[32,16,4,128]{3,2,1,0:T(4,128)(2,1)} %bitcast.14, bf16[24,32,4096]{2,1,0:T(8,128)(2,1)} %left_any.1, ...), custom_call_target="tpu_custom_call" | custom-call | tf_op jit(solution)/shard_map/fused/pallas_call | solution.py:478
  51.5 2.1 %copy.12 = bf16[32,4,2048]{2,1,0:T(4,128)(2,1)} copy(bf16[32,4,2048]{2,1,0:T(4,128)(2,1)} %bitcast.11) | data formatting | bytes 1048576
  (1 shorter events, 0.0 us)
Async XLA Ops:
  0.9 1.4 %copy-start = (s32[32]{0:T(128)}, s32[32]{0:T(128)S(1)}, u32[]{:S(2)}) copy-start(s32[32]{0:T(128)S(1)} %multiply_add_fusion.tgt) | copy-start | bytes 388
